TPU v7x, 32 devices: a whole 2x2x4 slice. The times are simulated.
32 devices in a mesh: grp: 4 (over y, x), leaf: 8 (over z, core).
Axes of the slice: x: 2, y: 2, z: 4, core: 2. Of those that a mesh axis runs over, the one named last changes fastest.
Arguments:
- basis: float32 [8, 65536], P(None, ('grp', 'leaf')), may hold values from -28 to 28
- roots: float32 [5], replicated, may hold values from 0.35 to 1
- near_blocks: bfloat16 [256, 6, 256, 256], P(('grp', 'leaf')), may hold values from -0.046875 to 0.046875
- near_ids: int32 [256, 6], P(('grp', 'leaf')), may hold values from 0 to 255, as said below
- leaf_basis: bfloat16 [256, 64, 256], P(('grp', 'leaf')), may hold values from -0.375 to 0.375
- far_coupling: bfloat16 [256, 8, 64, 64], P(('grp', 'leaf')), may hold values from -0.109375 to 0.109375
- far_ids: int32 [256, 8], P(('grp', 'leaf')), may hold values from 0 to 255, as said below
- transfer: bfloat16 [256, 64, 128], P(('grp', 'leaf')), may hold values from -0.5 to 0.5
- top_coupling: bfloat16 [128, 8, 128, 128], P(('grp', 'leaf')), may hold values from -0.078125 to 0.078125
- top_ids: int32 [128, 8], P(('grp', 'leaf')), may hold values from 0 to 127, as said below
Outputs:
- next_vector: float32 [65536], P(('grp', 'leaf'))
- hessen: float32 [9], replicated
Inputs may be any that keep to these rules, and one draw needn't show every extreme that they name: `near_ids`: row i starts with i itself; the others lie within 8 leaves of i. `far_ids`: every entry lies within 8 leaves of its row. `top_ids`: every entry lies within 4 parents of its row.
All inputs are finite; a program needn't handle non-finite values.
Results may differ from a plain program's by a relative error of at most 0.024.
Values may be sent and summed in bfloat16 or wider, within the bound.
A program may use at most 64 MiB of HBM per device.

v0:
```python
import jax
import jax.numpy as jnp
from jax import lax
from jax.sharding import PartitionSpec as P


def padded_2(value, sides, width):
    for axis, dim in sides:
        size, length = (lax.axis_size(axis), value.shape[dim])
        up = [(i, (i + 1) % size) for i in range(size - 1)]
        down = [(j, i) for i, j in up]
        last = lax.slice_in_dim(value, length - width, length, axis=dim)
        leading = lax.slice_in_dim(value, 0, width, axis=dim)
        before = lax.ppermute(last, axis, up)
        after = lax.ppermute(leading, axis, down)
        value = jnp.concatenate([before, value, after], axis=dim)
    return value


def apply_operator(
    field, near_blocks, near_ids, leaf_basis, far_coupling, far_ids, transfer, top_coupling, top_ids
):
    leaves_here = field.shape[0]
    width = field.shape[1]
    rank_size = leaf_basis.shape[1]
    prank_size = transfer.shape[2]
    parents_here = leaves_here // 2
    first = lax.axis_index(("grp", "leaf")) * leaves_here - leaves_here
    first_parent = lax.axis_index(("grp", "leaf")) * parents_here - parents_here
    rounded = field.astype(jnp.bfloat16)
    coeffs = jnp.einsum(
        "lra,la->lr", leaf_basis, rounded, preferred_element_type=jnp.float32
    ).astype(jnp.bfloat16)
    upward = jnp.einsum("lrp,lr->lp", transfer, coeffs, preferred_element_type=jnp.float32)
    upward = upward.reshape(parents_here, 2, prank_size).sum(1).astype(jnp.bfloat16)
    stacked = jnp.concatenate(
        [rounded, coeffs, upward.reshape(leaves_here, prank_size // 2)], axis=1
    )
    stack_pad = padded_2(stacked, ((("grp", "leaf"), 0),), leaves_here)
    padded = stack_pad[:, :width]
    coeff_pad = stack_pad[:, width : width + rank_size]
    parent_pad = stack_pad[:, width + rank_size :].reshape(stack_pad.shape[0] // 2, prank_size)
    nearby = padded[near_ids - first]
    near_term = jnp.einsum("lkab,lkb->la", near_blocks, nearby, preferred_element_type=jnp.float32)
    partners = coeff_pad[far_ids - first]
    leaf_sum = jnp.einsum(
        "lkrs,lks->lr", far_coupling, partners, preferred_element_type=jnp.float32
    )
    sources = parent_pad[top_ids - first_parent]
    top_sum = jnp.einsum(
        "pkab,pkb->pa", top_coupling, sources, preferred_element_type=jnp.float32
    ).astype(jnp.bfloat16)
    down = jnp.einsum(
        "lrp,lp->lr", transfer, jnp.repeat(top_sum, 2, axis=0), preferred_element_type=jnp.float32
    )
    local_coef = (leaf_sum + down).astype(jnp.bfloat16)
    far_term = jnp.einsum("lra,lr->la", leaf_basis, local_coef, preferred_element_type=jnp.float32)
    return 0.5 * field + near_term + far_term


def body(
    basis,
    roots,
    near_blocks,
    near_ids,
    leaf_basis,
    far_coupling,
    far_ids,
    transfer,
    top_coupling,
    top_ids,
):
    leaves_here = near_blocks.shape[0]
    width = near_blocks.shape[2]
    count = basis.shape[0]

    def operator(field):
        return apply_operator(
            field,
            near_blocks,
            near_ids,
            leaf_basis,
            far_coupling,
            far_ids,
            transfer,
            top_coupling,
            top_ids,
        )

    vectors = basis.reshape(count, leaves_here, width)
    product = vectors[count - 1]
    result = jnp.zeros_like(product)
    for index in range(roots.shape[0]):
        result = result + product / roots[index]
        if index < roots.shape[0] - 1:
            product = product - operator(product) / roots[index]
    image = operator(result)
    total = jnp.float32(leaves_here * width * lax.axis_size("grp") * lax.axis_size("leaf"))
    local_proj = jnp.einsum("mla,la->m", vectors, image, precision=lax.Precision.HIGHEST)
    hcoef = lax.psum(local_proj, ("grp", "leaf")) / total
    remain = image - jnp.einsum("m,mla->la", hcoef, vectors, precision=lax.Precision.HIGHEST)
    squared = lax.psum(jnp.sum(remain * remain), ("grp", "leaf")) / total
    beta = jnp.sqrt(squared + 1e-06)
    next_vector = (remain / beta).reshape(leaves_here * width)
    hessen = jnp.concatenate([hcoef, beta[None]])
    return (next_vector, hessen)


def solution(mesh):
    return jax.shard_map(
        body,
        mesh=mesh,
        in_specs=(
            P(None, ("grp", "leaf")),
            P(),
            P(("grp", "leaf"), None, None, None),
            P(("grp", "leaf"), None),
            P(("grp", "leaf"), None, None),
            P(("grp", "leaf"), None, None, None),
            P(("grp", "leaf"), None),
            P(("grp", "leaf"), None, None),
            P(("grp", "leaf"), None, None, None),
            P(("grp", "leaf"), None),
        ),
        out_specs=(P(("grp", "leaf")), P()),
        check_vma=False,
    )
```

profile of v0, /device:TPU:0, one launch (start us, length us, event | category | flops | bytes accessed | tf_op | source)
XLA Modules:
  0.0 196.1 jit_solution(3133048686699846669)
XLA Ops:
  0.7 1.0 slice_reduce_fusion
  1.7 1.2 fusion.39
  2.9 1.1 fusion.69
  4.1 1.3 collective-permute-start.1
  5.4 3.0 %collective-permute-start = (bf16[8,384]{1,0:T(8,128)(2,1)S(1)}, bf16[8,384]{1,0:T(8,128)(2,1)S(1)}, u32[]{:S(2)}, u32[]{:S(2)}) collective-permute-start(bf16[8,384]{1,0:T(8,128)(2,1)S(1)} %pad_maximum_fusion.5), channel_id=1, source_target_pairs={{0,1},{1,2},{2,3},{3,4},{4,5},{5,6},{6,7},{7,8},{8,9},{9,10},{10,1... | collective-permute-start | bytes 18440 | tf_op jit(solution)/shard_map/ppermute | solution.py:14
  9.3 1.5 fusion.90
  10.8 0.7 compare_select_fusion.1
  11.6 0.7 compare_select_fusion
  13.6 1.1 fusion.67
  15.3 1.6 fusion.8
  16.9 1.1 fusion.65
  18.7 4.5 %fusion.91 = f32[8,1,256,1]{2,1,3,0:T(1,128)S(1)} fusion(bf16[8,6,256,1]{2,3,1,0:T(2,128)(2,1)S(1)} %reshape.314, bf16[8,6,256,256]{3,2,1,0:T(8,128)(2,1)} %param.12), kind=kOutput, calls=%fused_computation.141 | convolution fusion | flops 6291456 | bytes 6324224 | tf_op jit(solution)/shard_map/lkab,lkb->la/dot_general | solution.py:44
  24.4 1.3 collective-permute-start.3
  25.7 5.2 %collective-permute-start.2 = (bf16[8,384]{1,0:T(8,128)(2,1)S(1)}, bf16[8,384]{1,0:T(8,128)(2,1)S(1)}, u32[]{:S(2)}, u32[]{:S(2)}) collective-permute-start(bf16[8,384]{1,0:T(8,128)(2,1)S(1)} %pad_maximum_fusion.6), channel_id=1, source_target_pairs={{0,1},{1,2},{2,3},{3,4},{4,5},{5,6},{6,7},{7,8},{8,9},{9,10},{10,1... | collective-permute-start | bytes 18440 | tf_op jit(solution)/shard_map/ppermute | solution.py:14
  30.9 0.8 collective-permute-done.2
  35.0 4.5 %fusion.92 = f32[8,1,256,1]{2,1,3,0:T(1,128)S(1)} fusion(bf16[8,6,256,1]{2,3,1,0:T(2,128)(2,1)S(1)} %reshape.316, bf16[8,6,256,256]{3,2,1,0:T(8,128)(2,1)} %param.12), kind=kOutput, calls=%fused_computation.142 | convolution fusion | flops 6291456 | bytes 6324224 | tf_op jit(solution)/shard_map/lkab,lkb->la/dot_general | solution.py:44
  39.5 0.7 fusion.81
  40.7 1.3 collective-permute-start.5
  42.0 4.2 %collective-permute-start.4 = (bf16[8,384]{1,0:T(8,128)(2,1)S(1)}, bf16[8,384]{1,0:T(8,128)(2,1)S(1)}, u32[]{:S(2)}, u32[]{:S(2)}) collective-permute-start(bf16[8,384]{1,0:T(8,128)(2,1)S(1)} %pad_maximum_fusion.7), channel_id=1, source_target_pairs={{0,1},{1,2},{2,3},{3,4},{4,5},{5,6},{6,7},{7,8},{8,9},{9,10},{10,1... | collective-permute-start | bytes 18440 | tf_op jit(solution)/shard_map/ppermute | solution.py:14
  46.3 0.8 collective-permute-done.4
  50.4 4.5 %fusion.93 = f32[8,1,256,1]{2,1,3,0:T(1,128)S(1)} fusion(bf16[8,6,256,1]{2,3,1,0:T(2,128)(2,1)S(1)} %reshape.318, bf16[8,6,256,256]{3,2,1,0:T(8,128)(2,1)} %param.12), kind=kOutput, calls=%fused_computation.143 | convolution fusion | flops 6291456 | bytes 6324224 | tf_op jit(solution)/shard_map/lkab,lkb->la/dot_general | solution.py:44
  56.1 1.3 collective-permute-start.7
  57.4 4.8 %collective-permute-start.6 = (bf16[8,384]{1,0:T(8,128)(2,1)S(1)}, bf16[8,384]{1,0:T(8,128)(2,1)S(1)}, u32[]{:S(2)}, u32[]{:S(2)}) collective-permute-start(bf16[8,384]{1,0:T(8,128)(2,1)S(1)} %pad_maximum_fusion.8), channel_id=1, source_target_pairs={{0,1},{1,2},{2,3},{3,4},{4,5},{5,6},{6,7},{7,8},{8,9},{9,10},{10,1... | collective-permute-start | bytes 18440 | tf_op jit(solution)/shard_map/ppermute | solution.py:14
  62.1 0.8 collective-permute-done.6
  66.2 4.5 %fusion.94 = f32[8,1,256,1]{2,1,3,0:T(1,128)S(1)} fusion(bf16[8,6,256,1]{2,3,1,0:T(2,128)(2,1)S(1)} %reshape.320, bf16[8,6,256,256]{3,2,1,0:T(8,128)(2,1)} %param.12), kind=kOutput, calls=%fused_computation.144 | convolution fusion | flops 6291456 | bytes 6324224 | tf_op jit(solution)/shard_map/lkab,lkb->la/dot_general | solution.py:44
  70.7 3.2 %fusion.79 = (bf16[8,256]{1,0:T(8,128)(2,1)S(1)}, f32[8,256]{1,0:T(8,128)S(1)}) fusion(f32[]{:T(128)} %bitcast.92, f32[8,1,256]{2,1,0:T(1,128)S(1)} %fusion.47, f32[8,1,256,1]{2,1,3,0:T(1,128)S(1)} %fusion.94, f32[]{:T(128)} %bitcast.69, f32[8,256]{1,0:T(8,128)S(1)} %get-tuple-element.5, f32[8,1,256]{2,1,0:T(1,128)S(1)} %fusion.53, ...), kind=kLoop, calls=%fused_computation.132 | loop fusion | flops 40960 | bytes 69652 | tf_op jit(solution)/shard_map/convert_element_type | solution.py:30
  74.5 1.3 collective-permute-start.9
  75.8 4.8 %collective-permute-start.8 = (bf16[8,384]{1,0:T(8,128)(2,1)S(1)}, bf16[8,384]{1,0:T(8,128)(2,1)S(1)}, u32[]{:S(2)}, u32[]{:S(2)}) collective-permute-start(bf16[8,384]{1,0:T(8,128)(2,1)S(1)} %pad_maximum_fusion.9), channel_id=1, source_target_pairs={{0,1},{1,2},{2,3},{3,4},{4,5},{5,6},{6,7},{7,8},{8,9},{9,10},{10,1... | collective-permute-start | bytes 18440 | tf_op jit(solution)/shard_map/ppermute | solution.py:14
  80.6 0.8 collective-permute-done.8
  84.7 4.5 %fusion.95 = f32[8,1,256,1]{2,1,3,0:T(1,128)S(1)} fusion(bf16[8,6,256,1]{2,3,1,0:T(2,128)(2,1)S(1)} %reshape.322, bf16[8,6,256,256]{3,2,1,0:T(8,128)(2,1)} %param.12), kind=kOutput, calls=%fused_computation.145 | convolution fusion | flops 6291456 | bytes 6324224 | tf_op jit(solution)/shard_map/lkab,lkb->la/dot_general | solution.py:44
  89.4 61.1 %psum.14 = f32[8]{0:T(128)S(1)} all-reduce(f32[8]{0:T(128)S(1)} %convolution_bitcast_fusion), channel_id=1, replica_groups=mesh['grp'=4,'leaf'=8] {'grp','leaf'}, use_global_device_ids=true, to_apply=%region_5.0 | all-reduce | flops 8 | bytes 64 | tf_op jit(solution)/shard_map/psum | solution.py:100
  151.3 42.9 %psum.15 = f32[]{:T(128)} all-reduce(f32[]{:T(128)} %multiply_reduce_fusion), channel_id=1, replica_groups=mesh['grp'=4,'leaf'=8] {'grp','leaf'}, use_global_device_ids=true, to_apply=%region_7.0 | all-reduce | flops 1 | bytes 8 | tf_op jit(solution)/shard_map/psum | solution.py:102
  (141 shorter events, 22.4 us)
Async XLA Ops:
  0.6 12.6 %copy-start = (bf16[4,8,128,128]{3,2,1,0:T(8,128)(2,1)S(1)}, bf16[4,8,128,128]{3,2,1,0:T(8,128)(2,1)}, u32[]{:S(2)}) copy-start(bf16[4,8,128,128]{3,2,1,0:T(8,128)(2,1)} %param.18) | copy-start | bytes 3145732
  0.6 23.2 %copy-start.1 = (bf16[8,64,256]{2,1,0:T(8,128)(2,1)S(1)}, bf16[8,64,256]{2,1,0:T(8,128)(2,1)}, u32[]{:S(2)}) copy-start(bf16[8,64,256]{2,1,0:T(8,128)(2,1)} %param.14) | copy-start | bytes 786436
  0.7 23.4 %copy-start.4 = (bf16[8,64,128]{2,1,0:T(8,128)(2,1)S(1)}, bf16[8,64,128]{2,1,0:T(8,128)(2,1)}, u32[]{:S(2)}) copy-start(bf16[8,64,128]{2,1,0:T(8,128)(2,1)} %param.17) | copy-start | bytes 393220
  1.7 32.8 %copy-start.3 = (bf16[8,8,64,64]{3,2,1,0:T(8,128)(2,1)S(1)}, bf16[8,8,64,64]{3,2,1,0:T(8,128)(2,1)}, u32[]{:S(2)}) copy-start(bf16[8,8,64,64]{3,2,1,0:T(8,128)(2,1)} %param.15) | copy-start | bytes 1572868
  4.1 8.2 %collective-permute-start.1 = (bf16[8,384]{1,0:T(8,128)(2,1)S(1)}, bf16[8,384]{1,0:T(8,128)(2,1)S(1)}, u32[]{:S(2)}, u32[]{:S(2)}) collective-permute-start(bf16[8,384]{1,0:T(8,128)(2,1)S(1)} %pad_maximum_fusion.5), channel_id=1, source_target_pairs={{1,0},{2,1},{3,2},{4,3},{5,4},{6,5},{7,6},{8,7},{9,8},{10,9},{11,1... | collective-permute-start | bytes 18440 | tf_op jit(solution)/shard_map/ppermute | solution.py:15
  5.4 6.9 %collective-permute-start = (bf16[8,384]{1,0:T(8,128)(2,1)S(1)}, bf16[8,384]{1,0:T(8,128)(2,1)S(1)}, u32[]{:S(2)}, u32[]{:S(2)}) collective-permute-start(bf16[8,384]{1,0:T(8,128)(2,1)S(1)} %pad_maximum_fusion.5), channel_id=1, source_target_pairs={{0,1},{1,2},{2,3},{3,4},{4,5},{5,6},{6,7},{7,8},{8,9},{9,10},{10,1... | collective-permute-start | bytes 18440 | tf_op jit(solution)/shard_map/ppermute | solution.py:14
  24.4 6.5 %collective-permute-start.3 = (bf16[8,384]{1,0:T(8,128)(2,1)S(1)}, bf16[8,384]{1,0:T(8,128)(2,1)S(1)}, u32[]{:S(2)}, u32[]{:S(2)}) collective-permute-start(bf16[8,384]{1,0:T(8,128)(2,1)S(1)} %pad_maximum_fusion.6), channel_id=1, source_target_pairs={{1,0},{2,1},{3,2},{4,3},{5,4},{6,5},{7,6},{8,7},{9,8},{10,9},{11,1... | collective-permute-start | bytes 18440 | tf_op jit(solution)/shard_map/ppermute | solution.py:15
  25.7 6.0 %collective-permute-start.2 = (bf16[8,384]{1,0:T(8,128)(2,1)S(1)}, bf16[8,384]{1,0:T(8,128)(2,1)S(1)}, u32[]{:S(2)}, u32[]{:S(2)}) collective-permute-start(bf16[8,384]{1,0:T(8,128)(2,1)S(1)} %pad_maximum_fusion.6), channel_id=1, source_target_pairs={{0,1},{1,2},{2,3},{3,4},{4,5},{5,6},{6,7},{7,8},{8,9},{9,10},{10,1... | collective-permute-start | bytes 18440 | tf_op jit(solution)/shard_map/ppermute | solution.py:14
  40.7 5.5 %collective-permute-start.5 = (bf16[8,384]{1,0:T(8,128)(2,1)S(1)}, bf16[8,384]{1,0:T(8,128)(2,1)S(1)}, u32[]{:S(2)}, u32[]{:S(2)}) collective-permute-start(bf16[8,384]{1,0:T(8,128)(2,1)S(1)} %pad_maximum_fusion.7), channel_id=1, source_target_pairs={{1,0},{2,1},{3,2},{4,3},{5,4},{6,5},{7,6},{8,7},{9,8},{10,9},{11,1... | collective-permute-start | bytes 18440 | tf_op jit(solution)/shard_map/ppermute | solution.py:15
  42.0 5.0 %collective-permute-start.4 = (bf16[8,384]{1,0:T(8,128)(2,1)S(1)}, bf16[8,384]{1,0:T(8,128)(2,1)S(1)}, u32[]{:S(2)}, u32[]{:S(2)}) collective-permute-start(bf16[8,384]{1,0:T(8,128)(2,1)S(1)} %pad_maximum_fusion.7), channel_id=1, source_target_pairs={{0,1},{1,2},{2,3},{3,4},{4,5},{5,6},{6,7},{7,8},{8,9},{9,10},{10,1... | collective-permute-start | bytes 18440 | tf_op jit(solution)/shard_map/ppermute | solution.py:14
  56.1 6.1 %collective-permute-start.7 = (bf16[8,384]{1,0:T(8,128)(2,1)S(1)}, bf16[8,384]{1,0:T(8,128)(2,1)S(1)}, u32[]{:S(2)}, u32[]{:S(2)}) collective-permute-start(bf16[8,384]{1,0:T(8,128)(2,1)S(1)} %pad_maximum_fusion.8), channel_id=1, source_target_pairs={{1,0},{2,1},{3,2},{4,3},{5,4},{6,5},{7,6},{8,7},{9,8},{10,9},{11,1... | collective-permute-start | bytes 18440 | tf_op jit(solution)/shard_map/ppermute | solution.py:15
  57.4 5.6 %collective-permute-start.6 = (bf16[8,384]{1,0:T(8,128)(2,1)S(1)}, bf16[8,384]{1,0:T(8,128)(2,1)S(1)}, u32[]{:S(2)}, u32[]{:S(2)}) collective-permute-start(bf16[8,384]{1,0:T(8,128)(2,1)S(1)} %pad_maximum_fusion.8), channel_id=1, source_target_pairs={{0,1},{1,2},{2,3},{3,4},{4,5},{5,6},{6,7},{7,8},{8,9},{9,10},{10,1... | collective-permute-start | bytes 18440 | tf_op jit(solution)/shard_map/ppermute | solution.py:14
  70.7 18.4 %copy-start.2 = (f32[8,2048]{1,0:T(8,128)S(1)}, f32[8,2048]{1,0:T(8,128)}, u32[]{:S(2)}) copy-start(f32[8,2048]{1,0:T(8,128)} %param.10) | copy-start | bytes 196612
  74.5 6.1 %collective-permute-start.9 = (bf16[8,384]{1,0:T(8,128)(2,1)S(1)}, bf16[8,384]{1,0:T(8,128)(2,1)S(1)}, u32[]{:S(2)}, u32[]{:S(2)}) collective-permute-start(bf16[8,384]{1,0:T(8,128)(2,1)S(1)} %pad_maximum_fusion.9), channel_id=1, source_target_pairs={{1,0},{2,1},{3,2},{4,3},{5,4},{6,5},{7,6},{8,7},{9,8},{10,9},{11,1... | collective-permute-start | bytes 18440 | tf_op jit(solution)/shard_map/ppermute | solution.py:15
  75.8 5.6 %collective-permute-start.8 = (bf16[8,384]{1,0:T(8,128)(2,1)S(1)}, bf16[8,384]{1,0:T(8,128)(2,1)S(1)}, u32[]{:S(2)}, u32[]{:S(2)}) collective-permute-start(bf16[8,384]{1,0:T(8,128)(2,1)S(1)} %pad_maximum_fusion.9), channel_id=1, source_target_pairs={{0,1},{1,2},{2,3},{3,4},{4,5},{5,6},{6,7},{7,8},{8,9},{9,10},{10,1... | collective-permute-start | bytes 18440 | tf_op jit(solution)/shard_map/ppermute | solution.py:14
where the time goes:
time: 197 us; the launch traced here: 196 us
  blocking collectives  104 us (53%)
  matrix products  34.9 us (18%)
  starting transfers between devices  28.4 us (14%)
  local copies, waits for them, and re-layouts  14.3 us (7%)
  other arithmetic  9.53 us (5%)
  waiting for transfers between devices  3.21 us (2%)
    psum x1, blocking collectives, body(): hcoef = lax.psum(local_proj, ('grp', 'leaf')) / total  61.1 us
    psum x1, blocking collectives, body(): squared = lax.psum(jnp.sum(remain * remain), ('grp', 'leaf')) / total  42.9 us
    dot_general x5, matrix products, apply_operator(): jnp.einsum('lkab,lkb->la', near_blocks, nearby, preferred_element_type=jn...  22.5 us
    ppermute x5, starting transfers between devices, padded_2(): before = lax.ppermute(last, axis, up)  22 us
    ppermute x5, starting transfers between devices, padded_2(): after = lax.ppermute(leading, axis, down)  6.44 us
    convert_element_type x6, other arithmetic, apply_operator(): rounded = field.astype(jnp.bfloat16)  5.23 us
  transfers between devices with their start and end apart: 10, of which 4 were waited for; matrix products, arithmetic and copies ran while one was open for 2% of the time, Pallas kernels for 0%

commit v1 on v0

v1 whole, which is shorter than its diff:
```python
import functools

import jax
import jax.numpy as jnp
from jax import lax
from jax.experimental import pallas as pl
from jax.experimental.pallas import tpu as pltpu
from jax.sharding import PartitionSpec as P

MESH = pl.DeviceIdType.MESH
F32 = jnp.float32
BF16 = jnp.bfloat16


def nt(a, b):
    return lax.dot_general(a, b, (((1,), (1,)), ((), ())), preferred_element_type=F32)


def nn(a, b):
    return lax.dot_general(a, b, (((1,), (0,)), ((), ())), preferred_element_type=F32)


def kernel(
    n_grp,
    n_leaf,
    basis,
    roots,
    near_hbm,
    near_ids,
    lb_hbm,
    fc_hbm,
    far_ids,
    tr_hbm,
    tc_hbm,
    top_ids,
    out,
    hess,
    near,
    lb,
    fc,
    fcc,
    tr,
    tc,
    halo,
    prod_buf,
    z_buf,
    slots,
    load_sem,
    near_sem,
    send_sem,
    recv_sem,
    red_sem,
):
    n_dev = n_grp * n_leaf
    count = basis.shape[0]
    leaves, n_near, width, _ = near.shape
    n_far, rank = fc.shape[1], fc.shape[2]
    n_top, prank = tc.shape[1], tc.shape[2]
    parents = tc.shape[0]
    steps = roots.shape[0]
    coefs = leaves * rank
    me = lax.axis_index("grp") * n_leaf + lax.axis_index("leaf")

    def place(index):
        return (index // n_leaf, index % n_leaf)

    right = lax.rem(me + 1, n_dev)
    left = lax.rem(me + n_dev - 1, n_dev)

    lb_copy = pltpu.make_async_copy(lb_hbm, lb, load_sem.at[0])
    tr_copy = pltpu.make_async_copy(tr_hbm, tr, load_sem.at[1])
    fc_copy = pltpu.make_async_copy(fc_hbm, fc, load_sem.at[2])
    tc_copy = pltpu.make_async_copy(tc_hbm, tc, load_sem.at[3])
    near_copies = [
        pltpu.make_async_copy(near_hbm.at[i], near.at[i], near_sem.at[i]) for i in range(leaves)
    ]
    lb_copy.start()
    tr_copy.start()
    fc_copy.start()
    tc_copy.start()
    for copy in near_copies:
        copy.start()

    barrier = pltpu.get_barrier_semaphore()

    def greet(d, carry):
        pl.semaphore_signal(
            barrier, inc=1, device_id=place(lax.rem(me + d, n_dev)), device_id_type=MESH
        )
        return carry

    lax.fori_loop(1, n_dev, greet, 0)

    for i in range(leaves):
        prod_buf[i : i + 1, :] = basis[count - 1 : count, i * width : (i + 1) * width]
    z_buf[...] = jnp.zeros_like(z_buf)

    def iota(shape, dim):
        return lax.broadcasted_iota(jnp.int32, shape, dim)

    cands = 4 * leaves

    def onehots(columns):
        return [jnp.where(c == iota((leaves, cands), 1), 1.0, 0.0).astype(F32) for c in columns]

    base = me * leaves - leaves
    nid = near_ids[...] - base
    near_hot = jnp.concatenate(onehots([nid[:, k : k + 1] for k in range(1, n_near)]), 0)
    near_hot = near_hot.astype(BF16)
    fid = far_ids[...] - base
    far_hot = jnp.concatenate(onehots([fid[:, k : k + 1] for k in range(n_far)]), 0).astype(BF16)
    base_p = me * parents - parents
    tid = jnp.zeros((leaves, n_top), jnp.int32)
    for p in range(parents):
        tid = jnp.where(iota((leaves, n_top), 0) // 2 == p, top_ids[p : p + 1, :], tid)
    tid = (tid - base_p) * 2
    top_hot = jnp.concatenate(onehots([tid[:, k : k + 1] for k in range(n_top)]), 0).astype(BF16)

    gram = lax.dot_general(
        basis[...],
        basis[...],
        (((1,), (1,)), ((), ())),
        precision=lax.Precision.HIGHEST,
        preferred_element_type=F32,
    )

    row512 = iota((leaves, coefs), 0)
    block512 = iota((leaves, coefs), 1) // rank
    diag = row512 == block512
    row_l = iota((leaves, 2 * rank), 0)
    row_w = iota((leaves, width), 0)
    row_p = iota((leaves, prank), 0)
    low = iota((leaves, 2 * rank), 1) < rank

    fc_copy.wait()
    for k in range(n_far):
        for i in range(leaves):
            fcc[i * rank : (i + 1) * rank, k * rank : (k + 1) * rank] = fc[i, k]
    lb_copy.wait()
    tr_copy.wait()
    pl.semaphore_wait(barrier, n_dev - 1)

    def apply(step, field, first):
        xb = field.astype(BF16)
        full = jnp.where(diag, nt(xb, lb[...]), 0.0)
        part = full[:, 0 : 2 * rank]
        for v in range(1, leaves // 2):
            part = part + full[:, v * 2 * rank : (v + 1) * 2 * rank]
        part = part.astype(BF16).astype(F32)
        dup = part + pltpu.roll(part, rank, 1)
        swapped = jnp.where(
            row_l % 2 == 0, pltpu.roll(part, leaves - 1, 0), pltpu.roll(part, 1, 0)
        )
        pair = part + swapped
        lhs = jnp.concatenate(
            [jnp.where(row_l // 2 == v, pair, 0.0) for v in range(leaves // 2)], 1
        ).astype(BF16)
        up = nn(lhs, tr[...]).astype(BF16).astype(F32)
        halo[step, 1, :, 0:width] = xb.astype(F32)
        halo[step, 1, :, width : width + 2 * rank] = dup
        halo[step, 1, :, width + 2 * rank :] = up
        copies = []
        for side, target in ((0, right), (2, left)):
            copy = pltpu.make_async_remote_copy(
                src_ref=halo.at[step, 1],
                dst_ref=halo.at[step, side],
                send_sem=send_sem.at[step, side // 2],
                recv_sem=recv_sem.at[step, side // 2],
                device_id=place(target),
                device_id_type=MESH,
            )
            copy.start()
            copies.append(copy)
        acc = 0.5 * field
        own = []
        for i in range(leaves):
            if first:
                near_copies[i].wait()
            own.append(nt(xb, near[i, 0]))
        if first:
            tc_copy.wait()
        for copy in copies:
            copy.wait()
        cand = jnp.concatenate(
            [halo[step, 0], halo[step, 1], halo[step, 2], jnp.zeros_like(halo[step, 0])], 0
        ).astype(BF16)
        coef = nn(far_hot, cand[:, width : width + 2 * rank])
        par = nn(top_hot, cand[:, width + 2 * rank :])
        near_x = nn(near_hot, cand[:, 0:width])
        par_k = [par[k * leaves : (k + 1) * leaves].astype(BF16) for k in range(n_top)]
        srow = jnp.zeros((leaves, prank), F32)
        for p in range(parents):
            r = nt(par_k[0], tc[p, 0])
            for k in range(1, n_top):
                r = r + nt(par_k[k], tc[p, k])
            srow = jnp.where(row_p // 2 == p, r, srow)
        far_lhs = jnp.concatenate(
            [
                jnp.where(
                    low,
                    coef[2 * v * leaves : (2 * v + 1) * leaves],
                    coef[(2 * v + 1) * leaves : (2 * v + 2) * leaves],
                )
                for v in range(n_far // 2)
            ],
            1,
        ).astype(BF16)
        leaf_sum = nt(far_lhs, fcc[...])
        down = nt(srow.astype(BF16), tr[...])
        g = jnp.where(diag, leaf_sum + down, 0.0).astype(BF16)
        far = nn(g, lb[...])
        acc = acc + far
        xk = [near_x[k * leaves : (k + 1) * leaves].astype(BF16) for k in range(n_near - 1)]
        for i in range(leaves):
            r = own[i]
            for k in range(1, n_near):
                r = r + nt(xk[k - 1], near[i, k])
            acc = acc + jnp.where(row_w == i, r, 0.0)
        return acc

    def body(step, first):
        root = roots[step]
        prod = prod_buf[...]
        scaled = prod / root
        z = z_buf[...] + scaled
        z_buf[...] = z
        last = step == steps - 1
        field = jnp.where(last, z, prod)
        image = apply(step, field, first)
        prod_buf[...] = jnp.where(last, image, prod - image / root)

    body(0, True)

    def loop(step, carry):
        body(step, False)
        return carry

    lax.fori_loop(1, steps, loop, 0)

    w = prod_buf[...]
    proj = jnp.zeros((count, width), F32)
    for i in range(leaves):
        proj = proj + basis[:, i * width : (i + 1) * width] * w[i : i + 1, :]
    hcol = jnp.sum(proj, 1, keepdims=True)
    wcol = jnp.sum(w * w, 1, keepdims=True)
    lane = iota((count, 128), 1)
    rows = iota((count, 128), 0)
    tile = jnp.where(lane == count, hcol, 0.0) + jnp.where(lane == count + 1, wcol, 0.0)
    tile = tile + jnp.pad(gram, ((0, 0), (0, 128 - count)))
    slots[me] = tile

    def spread(d, carry):
        pltpu.make_async_remote_copy(
            src_ref=slots.at[me],
            dst_ref=slots.at[me],
            send_sem=red_sem.at[0],
            recv_sem=red_sem.at[1],
            device_id=place(lax.rem(me + d, n_dev)),
            device_id_type=MESH,
        ).start()
        return carry

    lax.fori_loop(1, n_dev, spread, 0)
    rest = pltpu.make_async_remote_copy(
        src_ref=slots.at[pl.ds(0, n_dev - 1)],
        dst_ref=slots.at[pl.ds(0, n_dev - 1)],
        send_sem=red_sem.at[0],
        recv_sem=red_sem.at[1],
        device_id=place(right),
        device_id_type=MESH,
    )
    rest.wait_recv()
    total = jnp.sum(slots[...], 0) * (1.0 / (leaves * width * n_dev))
    h = jnp.sum(jnp.where(lane == count, total, 0.0), 1, keepdims=True)
    ww = jnp.sum(jnp.where(lane == count + 1, total, 0.0), keepdims=True)
    hrow = jnp.sum(jnp.where(lane == rows, h, 0.0), 0, keepdims=True)
    quad = jnp.sum(h * (total * hrow), keepdims=True)
    hh = jnp.sum(h * h, keepdims=True)
    squared = jnp.maximum(ww - 2.0 * hh + quad, 0.0)
    beta = jnp.sqrt(squared + 1e-06)
    inverse = 1.0 / beta
    lane1 = iota((1, 128), 1)
    full = jnp.where(lane1 == count, beta, hrow)
    hess[...] = full[:, 0 : count + 1]
    for i in range(leaves):
        fit = jnp.sum(basis[:, i * width : (i + 1) * width] * h, 0, keepdims=True)
        out[:, i * width : (i + 1) * width] = (w[i : i + 1, :] - fit) * inverse
    rest.wait_send()


def make_body(n_grp, n_leaf):
    def body(
        basis,
        roots,
        near_blocks,
        near_ids,
        leaf_basis,
        far_coupling,
        far_ids,
        transfer,
        top_coupling,
        top_ids,
    ):
        leaves, rank, width = leaf_basis.shape
        prank = transfer.shape[2]
        count = basis.shape[0]
        steps = roots.shape[0]
        n_dev = n_grp * n_leaf
        payload = width + 2 * rank + prank
        vmem = pl.BlockSpec(memory_space=pltpu.VMEM)
        smem = pl.BlockSpec(memory_space=pltpu.SMEM)
        hbm = pl.BlockSpec(memory_space=pl.ANY)
        lb = leaf_basis.reshape(leaves * rank, width)
        tr = transfer.reshape(leaves * rank, prank)
        n_far = far_coupling.shape[1]
        out, hess = pl.pallas_call(
            functools.partial(kernel, n_grp, n_leaf),
            out_shape=(
                jax.ShapeDtypeStruct((1, leaves * width), F32),
                jax.ShapeDtypeStruct((1, count + 1), F32),
            ),
            in_specs=[vmem, smem, hbm, vmem, hbm, hbm, vmem, hbm, hbm, vmem],
            out_specs=(vmem, vmem),
            scratch_shapes=[
                pltpu.VMEM(near_blocks.shape, BF16),
                pltpu.VMEM(lb.shape, BF16),
                pltpu.VMEM(far_coupling.shape, BF16),
                pltpu.VMEM((leaves * rank, n_far * rank), BF16),
                pltpu.VMEM(tr.shape, BF16),
                pltpu.VMEM(top_coupling.shape, BF16),
                pltpu.VMEM((steps, 3, leaves, payload), F32),
                pltpu.VMEM((leaves, width), F32),
                pltpu.VMEM((leaves, width), F32),
                pltpu.VMEM((n_dev, count, 128), F32),
                pltpu.SemaphoreType.DMA((4,)),
                pltpu.SemaphoreType.DMA((leaves,)),
                pltpu.SemaphoreType.DMA((steps, 2)),
                pltpu.SemaphoreType.DMA((steps, 2)),
                pltpu.SemaphoreType.DMA((2,)),
            ],
            compiler_params=pltpu.CompilerParams(
                collective_id=0, has_side_effects=True, vmem_limit_bytes=48 * 1024 * 1024
            ),
        )(
            basis,
            roots,
            near_blocks,
            near_ids,
            lb,
            far_coupling,
            far_ids,
            tr,
            top_coupling,
            top_ids,
        )
        return out.reshape(leaves * width), hess.reshape(count + 1)

    return body


def solution(mesh):
    both = ("grp", "leaf")
    return jax.shard_map(
        make_body(mesh.shape["grp"], mesh.shape["leaf"]),
        mesh=mesh,
        in_specs=(
            P(None, both),
            P(),
            P(both, None, None, None),
            P(both, None),
            P(both, None, None),
            P(both, None, None, None),
            P(both, None),
            P(both, None, None),
            P(both, None, None, None),
            P(both, None),
        ),
        out_specs=(P(both), P()),
        check_vma=False,
    )
```

time: 197 us -> 58.4 us (0.30)
  blocking collectives: 104 us -> 0 us
  Pallas kernels: 0 us -> 48.4 us
  matrix products: 34.9 us -> 0 us
  starting transfers between devices: 28.4 us -> 0 us
  other arithmetic: 9.53 us -> 0 us
  local copies, waits for them, and re-layouts: 14.3 us -> 8.95 us
  waiting for transfers between devices: 3.21 us -> 0 us
    psum x2 -> x0, blocking collectives: 104 us -> none  [the longest x1 61.1 us: body(): hcoef = lax.psum(local_proj, ('grp', 'leaf')) / total]
    pallas_call x0 -> x1, Pallas kernels: none -> 48.4 us  [body(): pl.pallas_call(functools.partial(kernel, n_grp, n_leaf), out_shape=(jax.S...]
    dot_general x37 -> x0, matrix products: 34.9 us -> none  [the longest x5 22.5 us: apply_operator(): jnp.einsum('lkab,lkb->la', near_blocks, nearby, preferred_element_type=jn...]
    ppermute x10 -> x0, starting transfers between devices: 28.4 us -> none  [the longest x5 22 us: padded_2(): before = lax.ppermute(last, axis, up)]
    gather x20 -> x0, local copies, waits for them, and re-layouts: 9.65 us -> none  [the longest x10 3.47 us: apply_operator(): nearby = padded[near_ids - first]]
    unnamed x11 -> x20, local copies, waits for them, and re-layouts: 0.65 us -> 8.95 us
    convert_element_type x26 -> x0, other arithmetic: 5.34 us -> none  [the longest x6 5.23 us: apply_operator(): rounded = field.astype(jnp.bfloat16)]
    ppermute x10 -> x0, waiting for transfers between devices: 3.21 us -> none  [the longest x5 3.19 us: padded_2(): before = lax.ppermute(last, axis, up)]
  transfers between devices with their start and end apart: 10 -> 0, of which waited for: 4 -> 0; matrix products, arithmetic and copies ran while one was open for 2% -> 0% of each run, Pallas kernels for 0% -> 0%
where the time goes in v1:
time: 58.4 us; the launch traced here: 58 us
  Pallas kernels  48.4 us (83%)
  local copies, waits for them, and re-layouts  8.95 us (15%)
  between operations  0.66 us (1%)
    pallas_call x1, Pallas kernels, body(): pl.pallas_call(functools.partial(kernel, n_grp, n_leaf), out_shape=(jax.S...  48.4 us
    unnamed x20, local copies, waits for them, and re-layouts  8.95 us

profile of v1, /device:TPU:0, one launch (start us, length us, event | category | flops | bytes accessed | tf_op | source)
XLA Modules:
  0.0 58.0 jit_solution(1529397592560789706)
XLA Ops:
  0.6 0.0 copy-start
  0.6 1.2 %copy-done = bf16[8,8,64,64]{3,2,1,0:T(8,128)(2,1)S(1)} copy-done((bf16[8,8,64,64]{3,2,1,0:T(8,128)(2,1)S(1)}, bf16[8,8,64,64]{3,2,1,0:T(8,128)(2,1)}, u32[]{:S(2)}) %copy-start) | copy-done | bytes 524312
  1.9 0.0 copy-start.1
  1.9 1.2 %copy-done.1 = bf16[4,8,128,128]{3,2,1,0:T(8,128)(2,1)S(1)} copy-done((bf16[4,8,128,128]{3,2,1,0:T(8,128)(2,1)S(1)}, bf16[4,8,128,128]{3,2,1,0:T(8,128)(2,1)}, u32[]{:S(2)}) %copy-start.1) | copy-done | bytes 1048600
  3.1 0.0 copy-start.2
  3.1 0.9 %copy-done.2 = bf16[8,64,256]{2,1,0:T(8,128)(2,1)S(1)} copy-done((bf16[8,64,256]{2,1,0:T(8,128)(2,1)S(1)}, bf16[8,64,256]{2,1,0:T(8,128)(2,1)}, u32[]{:S(2)}) %copy-start.2) | copy-done | bytes 262168
  4.0 0.0 copy-start.3
  4.0 0.9 %copy-done.3 = bf16[8,64,128]{2,1,0:T(8,128)(2,1)S(1)} copy-done((bf16[8,64,128]{2,1,0:T(8,128)(2,1)S(1)}, bf16[8,64,128]{2,1,0:T(8,128)(2,1)}, u32[]{:S(2)}) %copy-start.3) | copy-done | bytes 131096
  4.9 0.0 copy-start.4
  4.9 0.8 %copy-done.4 = f32[8,2048]{1,0:T(8,128)S(1)} copy-done((f32[8,2048]{1,0:T(8,128)S(1)}, f32[8,2048]{1,0:T(8,128)}, u32[]{:S(2)}) %copy-start.4) | copy-done | bytes 65560
  5.8 0.0 copy-start.5
  5.8 0.7 %copy-done.5 = s32[8,6]{1,0:T(8,128)S(1)} copy-done((s32[8,6]{1,0:T(8,128)S(1)}, s32[8,6]{1,0:T(8,128)}, u32[]{:S(2)}) %copy-start.5) | copy-done | bytes 216
  6.5 0.0 copy-start.6
  6.5 0.7 %copy-done.6 = s32[8,8]{1,0:T(8,128)S(1)} copy-done((s32[8,8]{1,0:T(8,128)S(1)}, s32[8,8]{1,0:T(8,128)}, u32[]{:S(2)}) %copy-start.6) | copy-done | bytes 280
  7.2 0.0 copy-start.7
  7.2 0.7 %copy-done.7 = s32[4,8]{1,0:T(4,128)S(1)} copy-done((s32[4,8]{1,0:T(4,128)S(1)}, s32[4,8]{1,0:T(4,128)}, u32[]{:S(2)}) %copy-start.7) | copy-done | bytes 152
  7.8 0.0 copy-start.8
  7.8 0.7 %copy-done.8 = f32[5]{0:T(128)S(1)} copy-done((f32[5]{0:T(128)S(1)}, f32[5]{0:T(128)}, u32[]{:S(2)}) %copy-start.8) | copy-done | bytes 44
  8.5 48.4 %shard_map.113 = (f32[1,2048]{1,0:T(1,128)S(1)}, f32[1,9]{1,0:T(1,128)S(1)}) custom-call(f32[8,2048]{1,0:T(8,128)S(1)} %copy-done.4, f32[5]{0:T(128)S(1)} %copy-done.8, bf16[8,6,256,256]{3,2,1,0:T(8,128)(2,1)} %near_hbm.1, s32[8,6]{1,0:T(8,128)S(1)} %copy-done.5, bf16[512,256]{1,0:T(8,128)(2,1)S(1)} %bitcast.4, bf16[8,8,64,64]{3,2,1,0:T(8,128)(2,1)S(1)} %copy-done, ...), custom_call_target="tpu_custom_call" | custom-call | tf_op jit(solution)/shard_map/pallas_call | solution.py:316
  56.9 0.6 %copy.14 = f32[2048]{0:T(1024)} copy(f32[2048]{0:T(1024)S(1)} %bitcast.6) | data formatting | bytes 16384
  57.5 0.5 copy.15
Async XLA Ops:
  0.6 1.2 %copy-start = (bf16[8,8,64,64]{3,2,1,0:T(8,128)(2,1)S(1)}, bf16[8,8,64,64]{3,2,1,0:T(8,128)(2,1)}, u32[]{:S(2)}) copy-start(bf16[8,8,64,64]{3,2,1,0:T(8,128)(2,1)} %fc_hbm.1) | copy-start | bytes 1572868
  1.9 1.2 %copy-start.1 = (bf16[4,8,128,128]{3,2,1,0:T(8,128)(2,1)S(1)}, bf16[4,8,128,128]{3,2,1,0:T(8,128)(2,1)}, u32[]{:S(2)}) copy-start(bf16[4,8,128,128]{3,2,1,0:T(8,128)(2,1)} %tc_hbm.1) | copy-start | bytes 3145732
  3.1 0.9 %copy-start.2 = (bf16[8,64,256]{2,1,0:T(8,128)(2,1)S(1)}, bf16[8,64,256]{2,1,0:T(8,128)(2,1)}, u32[]{:S(2)}) copy-start(bf16[8,64,256]{2,1,0:T(8,128)(2,1)} %param.14) | copy-start | bytes 786436
  4.0 0.9 %copy-start.3 = (bf16[8,64,128]{2,1,0:T(8,128)(2,1)S(1)}, bf16[8,64,128]{2,1,0:T(8,128)(2,1)}, u32[]{:S(2)}) copy-start(bf16[8,64,128]{2,1,0:T(8,128)(2,1)} %param.17) | copy-start | bytes 393220
  4.9 0.8 %copy-start.4 = (f32[8,2048]{1,0:T(8,128)S(1)}, f32[8,2048]{1,0:T(8,128)}, u32[]{:S(2)}) copy-start(f32[8,2048]{1,0:T(8,128)} %basis.1) | copy-start | bytes 196612
  5.8 0.7 %copy-start.5 = (s32[8,6]{1,0:T(8,128)S(1)}, s32[8,6]{1,0:T(8,128)}, u32[]{:S(2)}) copy-start(s32[8,6]{1,0:T(8,128)} %near_ids.1) | copy-start | bytes 580
  6.5 0.7 %copy-start.6 = (s32[8,8]{1,0:T(8,128)S(1)}, s32[8,8]{1,0:T(8,128)}, u32[]{:S(2)}) copy-start(s32[8,8]{1,0:T(8,128)} %far_ids.1) | copy-start | bytes 772
  7.2 0.7 %copy-start.7 = (s32[4,8]{1,0:T(4,128)S(1)}, s32[4,8]{1,0:T(4,128)}, u32[]{:S(2)}) copy-start(s32[4,8]{1,0:T(4,128)} %top_ids.1) | copy-start | bytes 388
  7.8 0.7 %copy-start.8 = (f32[5]{0:T(128)S(1)}, f32[5]{0:T(128)}, u32[]{:S(2)}) copy-start(f32[5]{0:T(128)} %roots.1) | copy-start | bytes 64
